TPU v7x, 32 devices: a whole 2x2x4 slice. The times are simulated.
32 devices in a mesh: dp: 8 (over z, y), ctx: 4 (over x, core).
Axes of the slice: x: 2, y: 2, z: 4, core: 2. Of those that a mesh axis runs over, the one named last changes fastest.
Arguments:
- projected: bfloat16 [8, 512, 3, 4096], P('dp', 'ctx'), may hold values from -6 to 6
- short_taps: float32 [3, 3, 4096], P(None, None, 'ctx'), may hold values from -3 to 3
- long_filter: bfloat16 [512, 4096], P('dp', 'ctx'), may hold values from -1.1 to 1.1
- skip_gain: float32 [4096], P('ctx'), may hold values from -4 to 4
Outputs:
- mixed: bfloat16 [8, 512, 4096], P('dp', 'ctx')
All inputs are finite; a program needn't handle non-finite values.
Results may differ from a plain program's by a relative error of at most 0.012.
Values may be sent and summed in bfloat16 or wider, within the bound.
A program may use at most 64 MiB of HBM per device.

v0:
```python
import math
import jax
import jax.numpy as jnp
from jax import lax
from jax.sharding import PartitionSpec as P

RADIX = 64
HIGH = lax.Precision.HIGHEST


def causal_short(extended, taps, kernel_size):
    row_count = extended.shape[0] - (kernel_size - 1)
    widened = extended.astype(jnp.float32)
    summed = jnp.zeros((row_count,) + widened.shape[1:], jnp.float32)
    for tap_index in range(kernel_size):
        offset = kernel_size - 1 - tap_index
        summed = summed + taps[tap_index] * widened[offset : offset + row_count]
    return (summed[:, 0].astype(jnp.bfloat16), (summed[:, 1] * summed[:, 2]).astype(jnp.bfloat16))


def dft_tables(length, radix_size):
    outer_size = 2 * length // radix_size
    total_size = outer_size * radix_size
    outer_range = jnp.arange(outer_size, dtype=jnp.int32)
    inner_range = jnp.arange(radix_size, dtype=jnp.int32)
    angle_one = (
        2.0
        * math.pi
        / outer_size
        * (outer_range[:, None] * outer_range[None, :] % outer_size).astype(jnp.float32)
    )
    angle_twist = (
        2.0
        * math.pi
        / total_size
        * (outer_range[:, None] * inner_range[None, :] % total_size).astype(jnp.float32)
    )
    angle_two = (
        2.0
        * math.pi
        / radix_size
        * (inner_range[:, None] * inner_range[None, :] % radix_size).astype(jnp.float32)
    )
    twist_cos = jnp.cos(angle_twist)[:, :, None]
    twist_sin = jnp.sin(angle_twist)[:, :, None]
    return (
        jnp.cos(angle_one),
        jnp.sin(angle_one),
        twist_cos,
        twist_sin,
        jnp.cos(angle_two),
        jnp.sin(angle_two),
    )


def forward_dft(signal, tables, radix_size):
    cos_one, sin_one, twist_cos, twist_sin, cos_two, sin_two = tables
    outer_size = cos_one.shape[0]
    half_size = outer_size // 2
    block_width = signal.shape[1]
    shaped = signal.reshape(half_size, radix_size * block_width)
    first_re = jnp.dot(cos_one[:, :half_size], shaped, precision=HIGH).reshape(
        outer_size, radix_size, block_width
    )
    first_im = -jnp.dot(sin_one[:, :half_size], shaped, precision=HIGH).reshape(
        outer_size, radix_size, block_width
    )
    second_re = first_re * twist_cos + first_im * twist_sin
    second_im = first_im * twist_cos - first_re * twist_sin
    spec_re = jnp.einsum("amc,mb->abc", second_re, cos_two, precision=HIGH) + jnp.einsum(
        "amc,mb->abc", second_im, sin_two, precision=HIGH
    )
    spec_im = jnp.einsum("amc,mb->abc", second_im, cos_two, precision=HIGH) - jnp.einsum(
        "amc,mb->abc", second_re, sin_two, precision=HIGH
    )
    return (spec_re, spec_im)


def inverse_dft(spec_re, spec_im, tables, radix_size):
    cos_one, sin_one, twist_cos, twist_sin, cos_two, sin_two = tables
    outer_size = cos_one.shape[0]
    half_size = outer_size // 2
    block_width = spec_re.shape[2]
    back_re = jnp.einsum("abc,mb->amc", spec_re, cos_two, precision=HIGH) - jnp.einsum(
        "abc,mb->amc", spec_im, sin_two, precision=HIGH
    )
    back_im = jnp.einsum("abc,mb->amc", spec_re, sin_two, precision=HIGH) + jnp.einsum(
        "abc,mb->amc", spec_im, cos_two, precision=HIGH
    )
    turned_re = (back_re * twist_cos - back_im * twist_sin).reshape(
        outer_size, radix_size * block_width
    )
    turned_im = (back_re * twist_sin + back_im * twist_cos).reshape(
        outer_size, radix_size * block_width
    )
    result = jnp.dot(cos_one[:half_size], turned_re, precision=HIGH) - jnp.dot(
        sin_one[:half_size], turned_im, precision=HIGH
    )
    return result.reshape(half_size * radix_size, block_width) / (outer_size * radix_size)


def long_convolve(gated_slab, filter_slab):
    length, channels = gated_slab.shape
    block_width = min(128, channels)
    tables = dft_tables(length, RADIX)

    def one_block(block_index, output):
        offset = block_index * block_width
        signal = lax.dynamic_slice_in_dim(gated_slab, offset, block_width, 1).astype(jnp.float32)
        kernel_block = lax.dynamic_slice_in_dim(filter_slab, offset, block_width, 1).astype(
            jnp.float32
        )
        sig_re, sig_im = forward_dft(signal, tables, RADIX)
        ker_re, ker_im = forward_dft(kernel_block, tables, RADIX)
        prod_re = sig_re * ker_re - sig_im * ker_im
        prod_im = sig_re * ker_im + sig_im * ker_re
        result = inverse_dft(prod_re, prod_im, tables, RADIX)
        return lax.dynamic_update_slice_in_dim(output, result, offset, 1)

    return lax.fori_loop(
        0, channels // block_width, one_block, jnp.zeros((length, channels), jnp.float32)
    )


def make_response(gated_slab, filter_slab, skip_gain):
    long_part = long_convolve(gated_slab, filter_slab)
    return (long_part + skip_gain * gated_slab.astype(jnp.float32)).astype(jnp.bfloat16)


def combine_rows(query_part, response_part):
    return (query_part.astype(jnp.float32) * response_part.astype(jnp.float32)).astype(jnp.bfloat16)


def on_device(projected, short_taps, long_filter, skip_gain):
    kernel_size = short_taps.shape[0]
    tok_rows = projected[0]
    filter_slab = lax.all_gather(long_filter, "dp", axis=0, tiled=True)
    stream_slab = lax.all_to_all(tok_rows, "ctx", split_axis=2, concat_axis=0, tiled=True)
    extended = jnp.pad(stream_slab, ((kernel_size - 1, 0), (0, 0), (0, 0)))
    query_slab, gated_slab = causal_short(extended, short_taps, kernel_size)
    response_slab = make_response(gated_slab, filter_slab, skip_gain)
    mixed = lax.all_to_all(
        combine_rows(query_slab, response_slab), "ctx", split_axis=0, concat_axis=1, tiled=True
    )
    return mixed[None]


def solution(mesh):
    return jax.shard_map(
        on_device,
        mesh=mesh,
        in_specs=(P("dp", "ctx", None, None), P(None, None, "ctx"), P("dp", "ctx"), P("ctx")),
        out_specs=P("dp", "ctx", None),
        check_vma=False,
    )
```

profile of v0, /device:TPU:0, one launch (start us, length us, event | category | flops | bytes accessed | tf_op | source)
XLA Modules:
  0.0 225.1 jit_solution(1443863807638157853)
XLA Ops:
  6.5 7.2 %copy.33 = bf16[1,128,3,4096]{1,2,3,0:T(4,128)(2,1)} copy(bf16[1,128,3,4096]{3,1,2,0:T(8,128)(2,1)} %param.6) | data formatting | bytes 6291456 | tf_op args[0]
  13.8 5.0 %all-to-all-start = ((bf16[128,3,4096]{0,1,2:T(4,128)(2,1)}), bf16[128,3,4096]{0,1,2:T(4,128)(2,1)}, u32[]{:S(2)}, u32[]{:S(2)}) async-start(bf16[128,3,4096]{0,1,2:T(4,128)(2,1)} %bitcast.224), calls=%async_computation | async-start | bytes 8388608 | tf_op jit(solution)/shard_map/all_to_all | solution.py:138
  19.6 48.0 %all-to-all-done = bf16[128,3,4096]{0,1,2:T(4,128)(2,1)} async-done(((bf16[128,3,4096]{0,1,2:T(4,128)(2,1)}), bf16[128,3,4096]{0,1,2:T(4,128)(2,1)}, u32[]{:S(2)}, u32[]{:S(2)}) %all-to-all-start) | async-done | bytes 3145760 | tf_op jit(solution)/shard_map/all_to_all | solution.py:138
  67.6 5.5 %copy.34 = bf16[4,128,3,1024]{3,1,0,2:T(8,128)(2,1)S(1)} copy(bf16[4,128,3,1024]{1,2,3,0:T(4,128)(2,1)} %bitcast.3) | data formatting | bytes 6291456 | tf_op jit(solution)/shard_map/all_to_all | solution.py:138
  73.1 0.9 pad_convert_fusion
  74.0 1.9 fusion.123
  75.9 2.6 %copy-done = f32[512,3,1024]{2,0,1:T(8,128)} copy-done((f32[512,3,1024]{2,0,1:T(8,128)}, f32[512,3,1024]{2,0,1:T(8,128)S(1)}, u32[]{:S(2)}) %copy-start) | copy-done | bytes 6291480
  78.6 1.3 fusion.128
  80.1 115.5 %while.15 = (s32[]{:T(128)}, f32[512,1024]{1,0:T(8,128)S(1)}, bf16[512,1024]{1,0:T(8,128)(2,1)}, f32[16,16]{1,0:T(8,128)S(1)}, f32[16,16]{1,0:T(8,128)S(1)}, /*i...) while((s32[]{:T(128)}, f32[512,1024]{1,0:T(8,128)S(1)}, ...), condition=%wide.region_1.2_spmd.clone.clone, body=%wide.region_0.1_spmd.clone.clone.sunk | while | flops 1288484864 | bytes 33853592 | solution.py:120
  80.3 1.0 constant_dynamic-slice_fusion.3
  84.6 0.8 convolution_subtract_fusion.6
  89.2 0.9 multiply_add_fusion.4
  92.3 0.9 multiply_add_fusion.5
  94.7 1.0 constant_dynamic-slice_fusion.3
  99.0 0.8 convolution_subtract_fusion.6
  102.1 0.8 convolution_add_fusion.5
  103.6 0.9 multiply_add_fusion.4
  106.7 0.9 multiply_add_fusion.5
  109.1 1.0 constant_dynamic-slice_fusion.3
  113.4 0.8 convolution_subtract_fusion.6
  116.5 0.8 convolution_add_fusion.5
  118.0 0.9 multiply_add_fusion.4
  121.1 0.9 multiply_add_fusion.5
  123.5 1.0 constant_dynamic-slice_fusion.3
  127.8 0.8 convolution_subtract_fusion.6
  130.9 0.8 convolution_add_fusion.5
  132.4 0.9 multiply_add_fusion.4
  135.5 0.9 multiply_add_fusion.5
  138.0 1.0 constant_dynamic-slice_fusion.3
  142.2 0.8 convolution_subtract_fusion.6
  145.3 0.8 convolution_add_fusion.5
  146.8 0.9 multiply_add_fusion.4
  149.9 0.9 multiply_add_fusion.5
  152.4 1.0 constant_dynamic-slice_fusion.3
  156.6 0.8 convolution_subtract_fusion.6
  161.2 0.9 multiply_add_fusion.4
  164.4 0.9 multiply_add_fusion.5
  166.8 1.0 constant_dynamic-slice_fusion.3
  171.1 0.8 convolution_subtract_fusion.6
  175.6 0.9 multiply_add_fusion.4
  178.8 0.9 multiply_add_fusion.5
  181.2 1.0 constant_dynamic-slice_fusion.3
  185.5 0.8 convolution_subtract_fusion.6
  190.0 0.9 multiply_add_fusion.4
  193.2 0.9 multiply_add_fusion.5
  195.6 3.8 %fusion.126 = bf16[512,1024]{1,0:T(8,128)(2,1)S(1)} fusion(f32[512,1024]{1,0:T(8,128)S(1)} %get-tuple-element.246, f32[512,3,1024]{2,0,1:T(8,128)} %copy-done, f32[1024]{0:T(1024)S(1)} %copy-done.2), kind=kLoop, calls=%fused_computation.151 | loop fusion | flops 5242880 | bytes 8392704 | tf_op jit(solution)/shard_map/convert_element_type | solution.py:131
  199.4 16.9 %all_to_all.34 = bf16[4,128,1024]{2,1,0:T(8,128)(2,1)S(1)} all-to-all(bf16[4,128,1024]{2,1,0:T(8,128)(2,1)S(1)} %bitcast.227), channel_id=1, replica_groups=mesh['dp'=8,'ctx'=4] {'ctx'}, dimensions={0} | all-to-all | bytes 2097152 | tf_op jit(solution)/shard_map/all_to_all | solution.py:142
  217.0 1.3 copy.36
  (208 shorter events, 83.7 us)
Async XLA Ops:
  13.8 5.8 %copy-start.1 = (f32[3,3,1024]{2,1,0:T(4,128)S(1)}, f32[3,3,1024]{2,1,0:T(4,128)}, u32[]{:S(2)}) copy-start(f32[3,3,1024]{2,1,0:T(4,128)} %param.7) | copy-start | bytes 110596
  13.8 53.8 %all-to-all-start = ((bf16[128,3,4096]{0,1,2:T(4,128)(2,1)}), bf16[128,3,4096]{0,1,2:T(4,128)(2,1)}, u32[]{:S(2)}, u32[]{:S(2)}) async-start(bf16[128,3,4096]{0,1,2:T(4,128)(2,1)} %bitcast.224), calls=%async_computation | async-start | bytes 8388608 | tf_op jit(solution)/shard_map/all_to_all | solution.py:138
  18.7 61.1 %all-gather.2.cloned.1.call-start = ((), (), s32[]{:S(2)}) async-start(), calls=%async_computation.2 | async-start | bytes 1179648 | tf_op jit(solution)/shard_map/all_gather | solution.py:137
  75.9 2.7 %copy-start = (f32[512,3,1024]{2,0,1:T(8,128)}, f32[512,3,1024]{2,0,1:T(8,128)S(1)}, u32[]{:S(2)}) copy-start(f32[512,3,1024]{2,0,1:T(8,128)S(1)} %fusion.123) | copy-start | bytes 18874372
  80.1 115.5 %copy-start.2 = (f32[1024]{0:T(1024)S(1)}, f32[1024]{0:T(1024)}, u32[]{:S(2)}) copy-start(f32[1024]{0:T(1024)} %param.9) | copy-start | bytes 12292
Sparse Core Ops, SparseCore 0:
  21.7 43.2 all-gather.1
where the time goes:
time: 226 us; the launch traced here: 225 us
  matrix products  96.6 us (43%)
  waiting for transfers between devices  48.7 us (22%)
  local copies, waits for them, and re-layouts  30.4 us (13%)
  blocking collectives  16.9 us (7%)
  between operations  13.5 us (6%)
  other arithmetic  11.9 us (5%)
  starting transfers between devices  5.02 us (2%)
    all_to_all x1, waiting for transfers between devices, on_device(): lax.all_to_all(tok_rows, 'ctx', split_axis=2, concat_axis=0, tiled=True)  48 us
    all_to_all x1, blocking collectives, on_device(): lax.all_to_all(combine_rows(query_slab, response_slab), 'ctx', split_axis...  16.9 us
    dot_general x16, matrix products, forward_dft(): jnp.einsum('amc,mb->abc', second_re, sin_two, precision=HIGH)  13.3 us
    dot_general x16, matrix products, forward_dft(): jnp.einsum('amc,mb->abc', second_im, sin_two, precision=HIGH)  12.1 us
    dot_general x16, matrix products, forward_dft(): jnp.einsum('amc,mb->abc', second_re, cos_two, precision=HIGH)  12 us
    dot_general x16, matrix products, forward_dft(): jnp.einsum('amc,mb->abc', second_im, cos_two, precision=HIGH)  12 us
    unnamed x7, local copies, waits for them, and re-layouts  9.88 us
    dynamic_slice x8, local copies, waits for them, and re-layouts, one_block(): lax.dynamic_slice_in_dim(filter_slab, offset, block_width, 1)  7.97 us
  transfers between devices with their start and end apart: 2, of which 1 were waited for; matrix products, arithmetic and copies ran while one was open for 4% of the time, Pallas kernels for 0%

commit v1 on v0

--- a/solution.py
+++ b/solution.py
@@ -6,6 +6,18 @@
 
 RADIX = 64
 HIGH = lax.Precision.HIGHEST
+
+
+def _map_chunk(tile_in, dimension_no, q_in):
+    main, now = (tile_in.shape[:dimension_no], tile_in.shape[dimension_no + 1 :])
+    near = tile_in.reshape(*main, q_in, -1, *now)
+    return jnp.moveaxis(near, dimension_no, 0)
+
+
+def outputs_supply_all(piece_in, d0):
+    step_out = list(piece_in.shape[1:])
+    step_out[d0] *= piece_in.shape[0]
+    return jnp.moveaxis(piece_in, 0, d0).reshape(step_out)
 
 
 def causal_short(extended, taps, kernel_size):
@@ -135,7 +147,24 @@
     kernel_size = short_taps.shape[0]
     tok_rows = projected[0]
     filter_slab = lax.all_gather(long_filter, "dp", axis=0, tiled=True)
-    stream_slab = lax.all_to_all(tok_rows, "ctx", split_axis=2, concat_axis=0, tiled=True)
+
+    def write_loads_up(across, view, own_rows, array_in):
+        all_rows = jax.lax.axis_size(across)
+        piece_out = jax.lax.axis_index(across)
+        odd, b_now = (all_rows, piece_out)
+        top = _map_chunk(view, own_rows, odd)
+        local_next = top
+        for dd in range(1, odd):
+            piece_next, value_now = ((b_now + dd) % odd, (b_now - dd) % odd)
+            e_now = lax.dynamic_index_in_dim(top, piece_next, 0)
+            arr_out = range(odd)
+            spare = jax.lax.ppermute(
+                e_now, across, list(map(lambda num: (num, (num + dd) % odd), arr_out))
+            )
+            local_next = lax.dynamic_update_slice_in_dim(local_next, spare, value_now, axis=0)
+        return outputs_supply_all(local_next, array_in)
+
+    stream_slab = write_loads_up("ctx", tok_rows, 2, 0)
     extended = jnp.pad(stream_slab, ((kernel_size - 1, 0), (0, 0), (0, 0)))
     query_slab, gated_slab = causal_short(extended, short_taps, kernel_size)
     response_slab = make_response(gated_slab, filter_slab, skip_gain)

time: 226 us -> 210 us (0.929)
  waiting for transfers between devices: 48.7 us -> 30.4 us
    all_to_all x1 -> x0, waiting for transfers between devices: 48 us -> none  [on_device(): lax.all_to_all(tok_rows, 'ctx', split_axis=2, concat_axis=0, tiled=True)]
    ppermute x0 -> x3, waiting for transfers between devices: none -> 30.4 us  [write_loads_up(): jax.lax.ppermute(e_now, across, list(map(lambda num: (num, (num + dd) % o...]
    dynamic_update_slice x0 -> x4, local copies, waits for them, and re-layouts: none -> 6.5 us  [write_loads_up(): lax.dynamic_update_slice_in_dim(local_next, spare, value_now, axis=0)]
    all_to_all x1 -> x0, local copies, waits for them, and re-layouts: 5.51 us -> none  [on_device(): lax.all_to_all(tok_rows, 'ctx', split_axis=2, concat_axis=0, tiled=True)]
    all_to_all x1 -> x0, starting transfers between devices: 4.98 us -> none  [on_device(): lax.all_to_all(tok_rows, 'ctx', split_axis=2, concat_axis=0, tiled=True)]
    ppermute x0 -> x3, starting transfers between devices: none -> 4.4 us  [write_loads_up(): jax.lax.ppermute(e_now, across, list(map(lambda num: (num, (num + dd) % o...]
    unnamed x7, local copies, waits for them, and re-layouts: 9.88 us -> 6.14 us
  transfers between devices with their start and end apart: 2 -> 4, of which waited for: 1 -> 3; matrix products, arithmetic and copies ran while one was open for 4% -> 6% of each run, Pallas kernels for 0% -> 0%
where the time goes in v1:
time: 210 us; the launch traced here: 209 us
  matrix products  96.6 us (46%)
  waiting for transfers between devices  30.4 us (14%)
  local copies, waits for them, and re-layouts  29.6 us (14%)
  blocking collectives  18.4 us (9%)
  other arithmetic  13.9 us (7%)
  between operations  13.6 us (6%)
  starting transfers between devices  4.41 us (2%)
  loops' own time  2.28 us (1%)
    ppermute x3, waiting for transfers between devices, write_loads_up(): jax.lax.ppermute(e_now, across, list(map(lambda num: (num, (num + dd) % o...  30.4 us
    all_to_all x1, blocking collectives, on_device(): lax.all_to_all(combine_rows(query_slab, response_slab), 'ctx', split_axis...  18.4 us
    dot_general x16, matrix products, forward_dft(): jnp.einsum('amc,mb->abc', second_re, sin_two, precision=HIGH)  13.3 us
    dot_general x16, matrix products, forward_dft(): jnp.einsum('amc,mb->abc', second_im, sin_two, precision=HIGH)  12.1 us
    dot_general x16, matrix products, forward_dft(): jnp.einsum('amc,mb->abc', second_re, cos_two, precision=HIGH)  12 us
    dot_general x16, matrix products, forward_dft(): jnp.einsum('amc,mb->abc', second_im, cos_two, precision=HIGH)  12 us
    dynamic_slice x8, local copies, waits for them, and re-layouts, one_block(): lax.dynamic_slice_in_dim(filter_slab, offset, block_width, 1)  7.97 us
    dot_general x8, matrix products, inverse_dft(): jnp.einsum('abc,mb->amc', spec_im, cos_two, precision=HIGH)  7.16 us
  transfers between devices with their start and end apart: 4, of which 3 were waited for; matrix products, arithmetic and copies ran while one was open for 6% of the time, Pallas kernels for 0%

profile of v1, /device:TPU:0, one launch (start us, length us, event | category | flops | bytes accessed | tf_op | source)
XLA Modules:
  0.0 209.2 jit_solution(10733066446679257167)
XLA Ops:
  6.5 3.5 %copy.51 = bf16[1,128,3,4096]{1,3,2,0:T(8,128)(2,1)S(1)} copy(bf16[1,128,3,4096]{3,1,2,0:T(8,128)(2,1)} %param.6) | data formatting | bytes 6291456 | tf_op args[0]
  10.0 1.5 dynamic-slice_bitcast_fusion
  12.0 2.5 %collective-permute-start.1 = (bf16[1,128,3,1024]{1,3,0,2:T(8,128)(2,1)}, bf16[1,128,3,1024]{1,3,0,2:T(8,128)(2,1)}, u32[]{:S(2)}, u32[]{:S(2)}) collective-permute-start(bf16[1,128,3,1024]{1,3,0,2:T(8,128)(2,1)} %get-tuple-element.348), channel_id=1, source_target_pairs={{0,2},{1,3},{2,0},{3,1},{4,6},{5,7},{6,4},{7,5},{8,10},{9,11},{10,... | collective-permute-start | bytes 2359304 | tf_op jit(solution)/shard_map/ppermute | solution.py:161
  14.5 1.4 collective-permute-start.2
  16.1 15.4 %collective-permute-done = bf16[1,128,3,1024]{1,3,0,2:T(8,128)(2,1)} collective-permute-done((bf16[1,128,3,1024]{1,3,0,2:T(8,128)(2,1)}, bf16[1,128,3,1024]{1,3,0,2:T(8,128)(2,1)}, u32[]{:S(2)}, u32[]{:S(2)}) %collective-permute-start) | collective-permute-done | bytes 786464 | tf_op jit(solution)/shard_map/ppermute | solution.py:161
  31.5 1.2 constant_dynamic-update-slice_fusion.3
  33.2 1.2 constant_dynamic-update-slice_fusion.2
  34.4 14.6 %collective-permute-done.2 = bf16[1,128,3,1024]{1,3,0,2:T(8,128)(2,1)} collective-permute-done((bf16[1,128,3,1024]{1,3,0,2:T(8,128)(2,1)}, bf16[1,128,3,1024]{1,3,0,2:T(8,128)(2,1)}, u32[]{:S(2)}, u32[]{:S(2)}) %collective-permute-start.2) | collective-permute-done | bytes 786464 | tf_op jit(solution)/shard_map/ppermute | solution.py:161
  49.0 1.2 constant_dynamic-update-slice_fusion.1
  50.2 2.8 %copy.58 = bf16[4,128,3,1024]{3,1,0,2:T(8,128)(2,1)} copy(bf16[4,128,3,1024]{1,3,0,2:T(8,128)(2,1)S(1)} %constant_dynamic-update-slice_fusion.1) | data formatting | bytes 6291456 | tf_op jit(solution)/shard_map/dynamic_update_slice | solution.py:164
  53.0 2.8 %pad_convert_fusion = f32[514,3,1024]{2,0,1:T(8,128)S(1)} fusion(bf16[512,3,1024]{2,0,1:T(8,128)(2,1)} %bitcast.235), kind=kLoop, calls=%fused_computation.146 | loop fusion | flops 1579008 | bytes 9461760 | tf_op jit(solution)/shard_map/convert_element_type | solution.py:25
  55.8 1.9 fusion.123
  57.7 2.7 %copy-done = f32[512,3,1024]{2,0,1:T(8,128)} copy-done((f32[512,3,1024]{2,0,1:T(8,128)}, f32[512,3,1024]{2,0,1:T(8,128)S(1)}, u32[]{:S(2)}) %copy-start) | copy-done | bytes 6291480
  60.4 1.3 fusion.128
  61.9 115.7 %while.15 = (s32[]{:T(128)}, f32[512,1024]{1,0:T(8,128)S(1)}, bf16[512,1024]{1,0:T(8,128)(2,1)}, f32[16,16]{1,0:T(8,128)S(1)}, f32[16,16]{1,0:T(8,128)S(1)}, /*i...) while((s32[]{:T(128)}, f32[512,1024]{1,0:T(8,128)S(1)}, ...), condition=%wide.region_1.2_spmd.clone.clone, body=%wide.region_0.1_spmd.clone.clone.sunk | while | flops 1288484864 | bytes 33853592 | solution.py:132
  62.1 1.0 constant_dynamic-slice_fusion.3
  66.4 0.8 convolution_subtract_fusion.6
  71.0 0.9 multiply_add_fusion.4
  74.1 0.9 multiply_add_fusion.5
  76.6 1.0 constant_dynamic-slice_fusion.3
  80.8 0.8 convolution_subtract_fusion.6
  85.4 0.9 multiply_add_fusion.4
  88.6 0.9 multiply_add_fusion.5
  91.0 1.0 constant_dynamic-slice_fusion.3
  95.3 0.8 convolution_subtract_fusion.6
  99.8 0.9 multiply_add_fusion.4
  103.0 0.9 multiply_add_fusion.5
  105.4 1.0 constant_dynamic-slice_fusion.3
  114.3 0.9 multiply_add_fusion.4
  117.4 0.9 multiply_add_fusion.5
  119.8 1.0 constant_dynamic-slice_fusion.3
  128.7 0.9 multiply_add_fusion.4
  131.8 0.9 multiply_add_fusion.5
  134.2 1.0 constant_dynamic-slice_fusion.3
  138.5 0.8 convolution_subtract_fusion.6
  143.1 0.9 multiply_add_fusion.4
  146.2 0.9 multiply_add_fusion.5
  148.6 1.0 constant_dynamic-slice_fusion.3
  152.9 0.8 convolution_subtract_fusion.6
  157.5 0.9 multiply_add_fusion.4
  160.6 0.9 multiply_add_fusion.5
  163.1 1.0 constant_dynamic-slice_fusion.3
  171.9 0.9 multiply_add_fusion.4
  175.1 0.9 multiply_add_fusion.5
  177.7 3.8 %fusion.126 = bf16[512,1024]{1,0:T(8,128)(2,1)S(1)} fusion(f32[512,1024]{1,0:T(8,128)S(1)} %get-tuple-element.246, f32[512,3,1024]{2,0,1:T(8,128)} %copy-done, f32[1024]{0:T(1024)S(1)} %copy-done.2), kind=kLoop, calls=%fused_computation.151 | loop fusion | flops 5242880 | bytes 8392704 | tf_op jit(solution)/shard_map/convert_element_type | solution.py:143
  181.5 18.4 %all_to_all.16 = bf16[4,128,1024]{2,1,0:T(8,128)(2,1)S(1)} all-to-all(bf16[4,128,1024]{2,1,0:T(8,128)(2,1)S(1)} %bitcast.237), channel_id=1, replica_groups=mesh['dp'=8,'ctx'=4] {'ctx'}, dimensions={0} | all-to-all | bytes 2097152 | tf_op jit(solution)/shard_map/all_to_all | solution.py:171
  200.0 0.8 copy.59
  200.8 1.6 broadcast_in_dim.5
  (216 shorter events, 88.6 us)
Async XLA Ops:
  6.5 55.1 %all-gather.2.cloned.1.call-start = ((), (), s32[]{:S(2)}) async-start(), calls=%async_computation.1 | async-start | bytes 1179648 | tf_op jit(solution)/shard_map/all_gather | solution.py:149
  10.0 6.1 %copy-start.1 = (f32[3,3,1024]{2,1,0:T(4,128)S(1)}, f32[3,3,1024]{2,1,0:T(4,128)}, u32[]{:S(2)}) copy-start(f32[3,3,1024]{2,1,0:T(4,128)} %param.7) | copy-start | bytes 110596
  11.5 20.0 %collective-permute-start = (bf16[1,128,3,1024]{1,3,0,2:T(8,128)(2,1)}, bf16[1,128,3,1024]{1,3,0,2:T(8,128)(2,1)}, u32[]{:S(2)}, u32[]{:S(2)}) collective-permute-start(bf16[1,128,3,1024]{1,3,0,2:T(8,128)(2,1)} %get-tuple-element.349), channel_id=1, source_target_pairs={{0,1},{1,2},{2,3},{3,0},{4,5},{5,6},{6,7},{7,4},{8,9},{9,10},{10,1... | collective-permute-start | bytes 2359304 | tf_op jit(solution)/shard_map/ppermute | solution.py:161
  12.0 21.2 %collective-permute-start.1 = (bf16[1,128,3,1024]{1,3,0,2:T(8,128)(2,1)}, bf16[1,128,3,1024]{1,3,0,2:T(8,128)(2,1)}, u32[]{:S(2)}, u32[]{:S(2)}) collective-permute-start(bf16[1,128,3,1024]{1,3,0,2:T(8,128)(2,1)} %get-tuple-element.348), channel_id=1, source_target_pairs={{0,2},{1,3},{2,0},{3,1},{4,6},{5,7},{6,4},{7,5},{8,10},{9,11},{10,... | collective-permute-start | bytes 2359304 | tf_op jit(solution)/shard_map/ppermute | solution.py:161
  14.5 34.5 %collective-permute-start.2 = (bf16[1,128,3,1024]{1,3,0,2:T(8,128)(2,1)}, bf16[1,128,3,1024]{1,3,0,2:T(8,128)(2,1)}, u32[]{:S(2)}, u32[]{:S(2)}) collective-permute-start(bf16[1,128,3,1024]{1,3,0,2:T(8,128)(2,1)} %get-tuple-element.347), channel_id=1, source_target_pairs={{0,3},{1,0},{2,1},{3,2},{4,7},{5,4},{6,5},{7,6},{8,11},{9,8},{10,9... | collective-permute-start | bytes 2359304 | tf_op jit(solution)/shard_map/ppermute | solution.py:161
  57.7 2.7 %copy-start = (f32[512,3,1024]{2,0,1:T(8,128)}, f32[512,3,1024]{2,0,1:T(8,128)S(1)}, u32[]{:S(2)}) copy-start(f32[512,3,1024]{2,0,1:T(8,128)S(1)} %fusion.123) | copy-start | bytes 18874372
  61.9 115.8 %copy-start.2 = (f32[1024]{0:T(1024)S(1)}, f32[1024]{0:T(1024)}, u32[]{:S(2)}) copy-start(f32[1024]{0:T(1024)} %param.9) | copy-start | bytes 12292
Sparse Core Ops, SparseCore 0:
  16.1 40.3 all-gather.1
